TPU v7x, 32 devices: a whole 2x2x4 slice. The times are simulated.
32 devices in a mesh: dp: 4 (over x, core), expert: 8 (over z, y).
Axes of the slice: x: 2, y: 2, z: 4, core: 2. Of those that a mesh axis runs over, the one named last changes fastest.
Arguments:
- dense_weights: bfloat16 [3, 5632, 2048], P(None, 'dp', 'expert'), may hold values from -0.125 to 0.125
- tokens: bfloat16 [1024, 2048], P('expert'), may hold values from -6 to 6
- cotangent: bfloat16 [1024, 2048], P('expert'), may hold values from -6 to 6
- routes: int32 [1024, 4], P('expert'), may hold values from 0 to 7, all different within a row; in each aligned block of 128 rows (0 to 127, 128 to 255, ...) at most 80 rows name the same one
- route_gates: float32 [1024, 4], P('expert'), may hold values from 0.2 to 1
- unit_perm: int32 [2, 5632], replicated, may hold values from 0 to 5631, as said below
- slab_owner: int32 [8], replicated, may hold values from 0 to 7, each once
Outputs:
- mixed: bfloat16 [1024, 2048], P('expert', 'dp')
- token_grad: bfloat16 [1024, 2048], P('expert', 'dp')
- expert_grad: bfloat16 [8, 3, 1408, 2048], P('expert', None, 'dp')
Inputs may be any that keep to these rules, and one draw needn't show every extreme that they name: `unit_perm`: each row is a permutation of the 5632 units. In every row, for every slab s and share g, the 352 positions s * 1408 + g * 352 up to s * 1408 + (g + 1) * 352 - 1 hold exactly 88 units of each block of 1408 consecutive units. `slab_owner`: each slab number c * 4 + s is owned by exactly one expert. `routes`: each row names 4 different experts. In each aligned block of 128 rows no expert is named more than 80 times, a bound that some block reaches.
All inputs are finite; a program needn't handle non-finite values.
Results may differ from a plain program's by a relative error of at most 0.013.
Values may be sent and summed in bfloat16 or wider, within the bound.
A program may use at most 128 MiB of HBM per device.

v0:
```python
import jax
import jax.numpy as jnp
from jax import lax
from jax.sharding import PartitionSpec as P

FF = 5632
EH = 1408


def silu_parts(preact):
    sigmoid_value = jax.nn.sigmoid(preact)
    return (preact * sigmoid_value, sigmoid_value * (1.0 + preact * (1.0 - sigmoid_value)))


def contract_last(left_side, right_side):
    return lax.dot_general(
        left_side, right_side, (((1,), (1,)), ((), ())), preferred_element_type=jnp.float32
    )


def contract_first(left_side, right_side):
    return lax.dot_general(
        left_side, right_side, (((0,), (0,)), ((), ())), preferred_element_type=jnp.float32
    )


def widen_rounded(values):
    return lax.optimization_barrier(values).astype(jnp.float32)


def body(dense_weights, tokens, cotangent, routes, route_gates, unit_perm, slab_owner):
    dp_count = lax.axis_size("dp")
    expert_count = lax.axis_size("expert")
    my_row = lax.axis_index("dp")
    my_col = lax.axis_index("expert")
    block_weights = lax.all_gather(dense_weights, "expert", axis=2, tiled=True)
    block_units = block_weights.shape[1]
    units_share = EH // dp_count
    pick_count = units_share // dp_count
    slab_count = FF // EH
    owned_slab = slab_owner[my_col]
    copy_id = owned_slab // slab_count
    slab_start = owned_slab % slab_count * EH
    shares = lax.dynamic_slice(unit_perm, (copy_id, slab_start), (1, EH)).reshape(
        dp_count, units_share
    )
    sort_order = jnp.argsort(shares // block_units, axis=1, stable=True)
    ordered = jnp.take_along_axis(shares, sort_order, axis=1).reshape(
        dp_count, dp_count, pick_count
    )
    my_units = lax.dynamic_index_in_dim(ordered, my_row, 1, keepdims=False) - my_row * block_units
    outgoing = jnp.take(block_weights, my_units.reshape(-1), axis=1)
    arrived = lax.all_to_all(outgoing, "dp", split_axis=1, concat_axis=1, tiled=True)
    my_order = lax.dynamic_index_in_dim(sort_order, my_row, 0, keepdims=False)
    expert_weights = jnp.take(arrived, jnp.argsort(my_order), axis=1)
    tok_rows = tokens.shape[0]
    route_count = routes.shape[1]
    copies = tok_rows * route_count
    capacity = copies * 5 // (4 * expert_count)
    flat_routes = routes.reshape(-1)
    onehot = (flat_routes[:, None] == jnp.arange(expert_count, dtype=jnp.int32)[None, :]).astype(
        jnp.int32
    )
    slot_rank = jnp.sum((jnp.cumsum(onehot, axis=0) - 1) * onehot, axis=1)
    slot_index = flat_routes * capacity + slot_rank
    source = (
        jnp.full((expert_count * capacity,), copies, jnp.int32)
        .at[slot_index]
        .set(jnp.arange(copies, dtype=jnp.int32))
    )
    filled = source < copies
    safe_rows = jnp.minimum(source, copies - 1)
    token_of = safe_rows // route_count
    pick_rows = jnp.where(filled, token_of, tok_rows)
    padded_tokens = jnp.concatenate([tokens, jnp.zeros((1, tokens.shape[1]), jnp.bfloat16)], axis=0)
    gate_of = jnp.where(filled, route_gates.reshape(-1)[safe_rows], jnp.zeros((), jnp.float32))
    send_x = padded_tokens[pick_rows]
    send_dy = (gate_of[:, None] * cotangent[token_of].astype(jnp.float32)).astype(jnp.bfloat16)
    recv_x, recv_dy = (
        lax.all_to_all(send_x, "expert", split_axis=0, concat_axis=0, tiled=True),
        lax.all_to_all(send_dy, "expert", split_axis=0, concat_axis=0, tiled=True),
    )
    w_gate = expert_weights[0]
    w_up = expert_weights[1]
    w_down = expert_weights[2]
    pre_gate = contract_last(recv_x, w_gate)
    pre_up = contract_last(recv_x, w_up)
    activation, silu_slope = silu_parts(pre_gate)
    hidden = (activation * pre_up).astype(jnp.bfloat16)
    out_part = jnp.dot(hidden, w_down, preferred_element_type=jnp.float32).astype(jnp.bfloat16)
    d_hidden = contract_last(recv_dy, w_down)
    d_gate = (d_hidden * pre_up * silu_slope).astype(jnp.bfloat16)
    d_up = (d_hidden * activation).astype(jnp.bfloat16)
    both_grads = jnp.concatenate([d_gate, d_up], axis=1)
    both_rows = jnp.concatenate([w_gate, w_up], axis=0)
    back_part = jnp.dot(both_grads, both_rows, preferred_element_type=jnp.float32).astype(
        jnp.bfloat16
    )
    weight_grads = jnp.stack(
        [
            contract_first(d_gate, recv_x),
            contract_first(d_up, recv_x),
            contract_first(hidden, recv_dy),
        ]
    ).astype(jnp.bfloat16)[None]
    shared_gate_w = block_weights[0]
    shared_up_w = block_weights[1]
    shared_down_w = block_weights[2]
    shared_gate = contract_last(tokens, shared_gate_w)
    shared_up = contract_last(tokens, shared_up_w)
    shared_act, shared_slope = silu_parts(shared_gate)
    shared_hidden = (shared_act * shared_up).astype(jnp.bfloat16)
    shared_out = jnp.dot(shared_hidden, shared_down_w, preferred_element_type=jnp.float32)
    shared_dh = contract_last(cotangent, shared_down_w)
    shared_dgate = (shared_dh * shared_up * shared_slope).astype(jnp.bfloat16)
    shared_dup = (shared_dh * shared_act).astype(jnp.bfloat16)
    shared_back = jnp.dot(
        shared_dgate, shared_gate_w, preferred_element_type=jnp.float32
    ) + jnp.dot(shared_dup, shared_up_w, preferred_element_type=jnp.float32)
    summed_out, summed_back = (
        lax.psum_scatter(
            widen_rounded(out_part).astype(jnp.bfloat16), "dp", scatter_dimension=1, tiled=True
        ).astype(jnp.float32),
        lax.psum_scatter(
            widen_rounded(back_part).astype(jnp.bfloat16), "dp", scatter_dimension=1, tiled=True
        ).astype(jnp.float32),
    )
    ret_out, ret_back = (
        lax.all_to_all(
            summed_out.astype(jnp.bfloat16), "expert", split_axis=0, concat_axis=0, tiled=True
        ).astype(summed_out.dtype),
        lax.all_to_all(
            summed_back.astype(jnp.bfloat16), "expert", split_axis=0, concat_axis=0, tiled=True
        ).astype(summed_back.dtype),
    )
    rows_out = ret_out[slot_index].reshape(tok_rows, route_count, -1)
    rows_back = ret_back[slot_index].reshape(tok_rows, route_count, -1)
    shared_slice, shared_grad = (
        lax.psum_scatter(
            shared_out.astype(jnp.bfloat16), "dp", scatter_dimension=1, tiled=True
        ).astype(jnp.float32),
        lax.psum_scatter(
            shared_back.astype(jnp.bfloat16), "dp", scatter_dimension=1, tiled=True
        ).astype(jnp.float32),
    )
    mixed = shared_slice + jnp.sum(route_gates[:, :, None] * rows_out, axis=1)
    token_grad = shared_grad + jnp.sum(rows_back, axis=1)
    return (mixed.astype(jnp.bfloat16), token_grad.astype(jnp.bfloat16), weight_grads)


def solution(mesh):
    in_specs = (
        P(None, "dp", "expert"),
        P("expert", None),
        P("expert", None),
        P("expert", None),
        P("expert", None),
        P(),
        P(),
    )
    out_specs = (P("expert", "dp"), P("expert", "dp"), P("expert", None, "dp", None))
    return jax.shard_map(body, mesh=mesh, in_specs=in_specs, out_specs=out_specs, check_vma=False)
```

profile of v0, /device:TPU:0, one launch (start us, length us, event | category | flops | bytes accessed | tf_op | source)
XLA Modules:
  0.0 804.3 jit_solution(1391486535818355225)
XLA Ops:
  7.2 12.2 %copy.24 = bf16[3,1408,256]{2,0,1:T(4,128)(2,1)} copy(bf16[3,1408,256]{2,1,0:T(8,128)(2,1)} %param.7) | data formatting | bytes 4325376 | tf_op args[0]
  21.8 2.4 scatter_custom_fusion
  24.3 4.3 gather_fusion.4
  28.7 4.1 gather_fusion
  32.9 7.8 all-to-all-start
  44.8 3.9 sort.34
  48.8 11.9 %gather_fusion.7 = s32[1408]{0:T(1024)S(1)} fusion(s32[4,352]{1,0:T(4,128)S(1)} %reshape.187, s32[1408]{0:T(1024)S(1)} %reshape.251), kind=kCustom, calls=%fused_computation.7 | custom fusion | bytes 22528 | tf_op jit(solution)/shard_map/jit(take_along_axis)/gather | solution.py:48
  62.3 430.4 %all-gather.2.cloned.1.call-done = bf16[3,1408,2048]{2,0,1:T(4,128)(2,1)} async-done(((bf16[3,1408,256]{2,0,1:T(4,128)(2,1)}), bf16[3,1408,2048]{2,0,1:T(4,128)(2,1)}) %all-gather.2.cloned.1.call-update) | async-done | bytes 17301520 | tf_op jit(solution)/shard_map/all_gather | solution.py:36
  492.7 21.0 %gather_fusion.1 = bf16[352,3,2048]{2,1,0:T(4,128)(2,1)} fusion(bf16[3,1408,2048]{2,0,1:T(4,128)(2,1)} %all-gather.2.cloned.1.call-done, s32[1024]{0:T(1024)S(1)} %pad_clamp_fusion.4), kind=kCustom, calls=%fused_computation.1 | custom fusion | bytes 8652160 | tf_op jit(solution)/shard_map/jit(_take)/gather | solution.py:52
  513.7 7.9 select_bitcast_fusion.1
  521.5 1.5 copy-done.3
  523.0 5.1 all-to-all-start.1
  528.3 3.4 gather_fusion.5
  531.7 2.0 fusion.12
  533.7 59.6 %all-to-all-done.1 = bf16[3,352,2048]{2,0,1:T(4,128)(2,1)} async-done(((bf16[3,352,2048]{2,0,1:T(4,128)(2,1)}), bf16[3,352,2048]{2,0,1:T(4,128)(2,1)}, u32[]{:S(2)}, u32[]{:S(2)}) %all-to-all-start.1) | async-done | bytes 4325408 | tf_op jit(solution)/shard_map/all_to_all | solution.py:53
  593.2 4.6 all-to-all-start.3
  598.4 3.8 sort.35
  602.2 16.0 %gather_fusion.2 = bf16[352,3,2048]{2,1,0:T(4,128)(2,1)} fusion(bf16[3,352,2048]{2,0,1:T(4,128)(2,1)} %all-to-all-done.1, s32[1024]{0:T(1024)S(1)} %pad_clamp_fusion.3), kind=kCustom, calls=%fused_computation.2 | custom fusion | bytes 8652160 | tf_op jit(solution)/shard_map/jit(_take)/gather | solution.py:55
  618.3 5.4 select_bitcast_fusion
  623.7 6.4 fusion.61
  630.9 2.0 copy.71
  633.7 2.3 fusion.62
  636.0 21.1 %all-to-all-done.3 = bf16[8,80,2048]{2,1,0:T(8,128)(2,1)} async-done(((bf16[8,80,2048]{2,1,0:T(8,128)(2,1)}), bf16[8,80,2048]{2,1,0:T(8,128)(2,1)}, u32[]{:S(2)}, u32[]{:S(2)}) %all-to-all-start.3) | async-done | bytes 2621472 | tf_op jit(solution)/shard_map/all_to_all | solution.py:81
  657.1 3.7 fusion.34
  660.9 2.5 multiply_convert_fusion.1
  664.2 3.2 convolution_convert_fusion.1
  667.5 5.8 convolution_convert_fusion
  673.4 43.0 %fusion.60 = (bf16[1,1408,2048]{2,0,1:T(2,128)(2,1)}, bf16[1,1408,2048]{2,0,1:T(2,128)(2,1)}, bf16[1,1408,2048]{2,0,1:T(2,128)(2,1)}) fusion(bf16[3,1408,2048]{2,0,1:T(4,128)(2,1)} %all-gather.2.cloned.1.call-done), kind=kLoop, calls=%fused_computation.121 | loop fusion | bytes 34603008 | tf_op jit(solution)/shard_map/slice | solution.py:106
  716.4 8.5 %fusion.10 = f32[128,1408]{1,0:T(8,128)S(1)} fusion(bf16[128,2048]{1,0:T(8,128)(2,1)S(1)} %copy-done.11, bf16[1,1408,2048]{2,0,1:T(2,128)(2,1)} %get-tuple-element.11), kind=kOutput, calls=%fused_computation.19 | convolution fusion | flops 738197504 | bytes 7012352 | tf_op jit(solution)/shard_map/dot_general | solution.py:16
  724.9 8.1 %fusion = f32[128,1408]{1,0:T(8,128)S(1)} fusion(bf16[128,2048]{1,0:T(8,128)(2,1)S(1)} %copy-done, bf16[1,1408,2048]{2,0,1:T(2,128)(2,1)} %get-tuple-element.12), kind=kOutput, calls=%fused_computation.9 | convolution fusion | flops 738197504 | bytes 7012352 | tf_op jit(solution)/shard_map/dot_general | solution.py:16
  733.0 3.7 fusion.6
  736.7 4.1 fusion.4
  740.9 4.6 fusion.22
  745.6 4.2 all-to-all-start.2
  749.8 8.9 %fusion.25 = bf16[128,2048]{1,0:T(8,128)(2,1)} fusion(bf16[1,1408,2048]{2,0,1:T(2,128)(2,1)} %get-tuple-element.12, f32[128,1408]{1,0:T(8,128)S(1)} %fusion.6, f32[128,1408]{1,0:T(8,128)S(1)} %fusion.10), kind=kOutput, calls=%fused_computation.39 | convolution fusion | flops 739540992 | bytes 7733248 | tf_op jit(solution)/shard_map/dot_general | solution.py:113
  758.8 4.4 fusion.18
  763.2 3.1 all-to-all-done.2
  766.4 4.4 all-to-all-start.4
  770.8 2.4 fusion.16
  773.2 1.3 fusion.17
  774.5 2.3 pad_maximum_fusion
  778.1 1.6 gather_fusion.3
  781.0 6.5 all-to-all-done.4
  788.8 1.6 gather_fusion.6
  790.5 1.3 reshape.191
  791.8 1.8 reduce_sum.32
  794.4 1.6 add_convert_fusion
  796.0 1.6 add_convert_fusion.1
  (108 shorter events, 13.6 us)
Async XLA Ops:
  7.2 521.1 %copy-start = (bf16[128,2048]{1,0:T(8,128)(2,1)S(1)}, bf16[128,2048]{1,0:T(8,128)(2,1)}, u32[]{:S(2)}) copy-start(bf16[128,2048]{1,0:T(8,128)(2,1)} %param.9) | copy-start | bytes 1572868
  7.2 12.3 %copy-start.12 = (s32[128,4]{0,1:T(4,128)S(1)}, s32[128,4]{0,1:T(4,128)}, u32[]{:S(2)}) copy-start(s32[128,4]{0,1:T(4,128)} %param.10) | copy-start | bytes 6148
  7.2 12.9 %copy-start.13 = (f32[128,4]{0,1:T(4,128)S(1)}, f32[128,4]{0,1:T(4,128)}, u32[]{:S(2)}) copy-start(f32[128,4]{0,1:T(4,128)} %param.11) | copy-start | bytes 6148
  7.2 485.5 %all-gather.2.cloned.1.call-start = ((), (), s32[]{:S(2)}) async-start(), calls=%async_computation.9 | async-start | bytes 25952256 | tf_op jit(solution)/shard_map/all_gather | solution.py:36
  19.5 9.1 %copy-start.10 = (bf16[128,2048]{1,0:T(8,128)(2,1)S(1)}, bf16[128,2048]{1,0:T(8,128)(2,1)}, u32[]{:S(2)}) copy-start(bf16[128,2048]{1,0:T(8,128)(2,1)} %param.8) | copy-start | bytes 1572868
  32.9 7.8 copy-start.14
  32.9 488.7 %all-to-all-start = ((bf16[8,80,2048]{2,1,0:T(8,128)(2,1)}), bf16[8,80,2048]{2,1,0:T(8,128)(2,1)S(1)}, u32[]{:S(2)}, u32[]{:S(2)}) async-start(bf16[8,80,2048]{2,1,0:T(8,128)(2,1)} %bitcast.87), calls=%async_computation.1 | async-start | bytes 5242880 | tf_op jit(solution)/shard_map/all_to_all | solution.py:80
  521.5 1.5 copy-start.3
  523.0 70.2 %all-to-all-start.1 = ((bf16[3,352,2048]{2,0,1:T(4,128)(2,1)}), bf16[3,352,2048]{2,0,1:T(4,128)(2,1)}, u32[]{:S(2)}, u32[]{:S(2)}) async-start(bf16[3,352,2048]{2,0,1:T(4,128)(2,1)} %select_bitcast_fusion.1), calls=%async_computation.2 | async-start | bytes 11534336 | tf_op jit(solution)/shard_map/all_to_all | solution.py:53
  593.2 63.9 %all-to-all-start.3 = ((bf16[8,80,2048]{2,1,0:T(8,128)(2,1)}), bf16[8,80,2048]{2,1,0:T(8,128)(2,1)}, u32[]{:S(2)}, u32[]{:S(2)}) async-start(bf16[8,80,2048]{2,1,0:T(8,128)(2,1)} %fusion.12), calls=%async_computation.6 | async-start | bytes 5242880 | tf_op jit(solution)/shard_map/all_to_all | solution.py:81
  597.8 147.8 %reduce-scatter.7.cloned.1.call-start = ((), (), s32[]{:S(2)}) async-start(), calls=%async_computation.11 | async-start | bytes 3276800 | tf_op jit(solution)/shard_map/reduce_scatter | solution.py:121
  630.9 2.0 copy-start.7
  630.9 2.8 copy-start.4
  657.1 3.7 copy-start.5
  657.1 3.7 copy-start.8
  657.1 3.7 copy-start.17
  663.4 0.8 copy-start.15
  667.5 95.8 %reduce-scatter.11.cloned.1.call-start = ((), (), s32[]{:S(2)}) async-start(), calls=%async_computation.13 | async-start | bytes 3276800 | tf_op jit(solution)/shard_map/reduce_scatter | solution.py:124
  673.4 43.0 %copy-start.11 = (bf16[128,2048]{1,0:T(8,128)(2,1)S(1)}, bf16[128,2048]{1,0:T(8,128)(2,1)}, u32[]{:S(2)}) copy-start(bf16[128,2048]{1,0:T(8,128)(2,1)} %param.8) | copy-start | bytes 1572868
  673.4 121.0 %reduce-scatter.9.cloned.1.call-start = ((), (), s32[]{:S(2)}) async-start(), calls=%async_computation.12 | async-start | bytes 655360 | tf_op jit(solution)/shard_map/reduce_scatter | solution.py:142
  716.4 16.6 %copy-start.1 = (bf16[1,1408,2048]{2,0,1:T(2,128)(2,1)S(1)}, bf16[1,1408,2048]{2,0,1:T(2,128)(2,1)}, u32[]{:S(2)}) copy-start(bf16[1,1408,2048]{2,0,1:T(2,128)(2,1)} %get-tuple-element.13) | copy-start | bytes 17301508
  724.9 16.0 %slice-start = ((s8[11534336]{0:T(1024)(128)(4,1)}), s8[3145728]{0:T(1024)(128)(4,1)S(1)}, s32[]{:S(2)}) async-start(s8[11534336]{0:T(1024)(128)(4,1)} %bitcast.85), calls=%async_computation.14 | async-start | bytes 6291456
  733.0 7.8 slice-start.1
  736.7 4.1 slice-start.2
  745.6 20.8 %all-to-all-start.2 = ((bf16[8,80,512]{2,1,0:T(8,128)(2,1)}), bf16[8,80,512]{2,1,0:T(8,128)(2,1)}, u32[]{:S(2)}, u32[]{:S(2)}) async-start(bf16[8,80,512]{2,1,0:T(8,128)(2,1)} %bitcast.98), calls=%async_computation.4 | async-start | bytes 1310720 | tf_op jit(solution)/shard_map/all_to_all | solution.py:129
  749.8 46.2 %reduce-scatter.5.cloned.1.call-start = ((), (), s32[]{:S(2)}) async-start(), calls=%async_computation.10 | async-start | bytes 655360 | tf_op jit(solution)/shard_map/reduce_scatter | solution.py:139
  758.8 12.0 %copy-start.6 = (bf16[8,80,2048]{2,1,0:T(8,128)(2,1)S(1)}, bf16[8,80,2048]{2,1,0:T(8,128)(2,1)}, u32[]{:S(2)}) copy-start(bf16[8,80,2048]{2,1,0:T(8,128)(2,1)} %copy-done.3) | copy-start | bytes 7864324
  766.4 21.2 %all-to-all-start.4 = ((bf16[8,80,512]{2,1,0:T(8,128)(2,1)}), bf16[8,80,512]{2,1,0:T(8,128)(2,1)}, u32[]{:S(2)}, u32[]{:S(2)}) async-start(bf16[8,80,512]{2,1,0:T(8,128)(2,1)} %bitcast.97), calls=%async_computation.8 | async-start | bytes 1310720 | tf_op jit(solution)/shard_map/all_to_all | solution.py:132
  770.8 2.4 copy-start.16
  773.1 1.4 copy-start.9
  790.4 3.2 copy-start.2
Sparse Core Ops, SparseCore 0:
  19.6 473.0 all-gather.1
  667.6 32.6 reduce-scatter.6
  702.8 34.3 reduce-scatter.10
  745.7 19.4 reduce-scatter.8
  767.5 21.6 reduce-scatter.4
where the time goes:
time: 811 us; the launch traced here: 804 us
  waiting for transfers between devices  521 us (64%)
  local copies, waits for them, and re-layouts  140 us (17%)
  matrix products  63.6 us (8%)
  other arithmetic  35.6 us (4%)
  starting transfers between devices  26.8 us (3%)
  between operations  17.2 us (2%)
    all_gather x1, waiting for transfers between devices, body(): block_weights = lax.all_gather(dense_weights, 'expert', axis=2, tiled=True)  430 us
    all_to_all x1, waiting for transfers between devices, body(): lax.all_to_all(outgoing, 'dp', split_axis=1, concat_axis=1, tiled=True)  59.6 us
    slice x1, local copies, waits for them, and re-layouts, body(): shared_gate_w = block_weights[0]  43 us
    dot_general x6, matrix products, contract_last(): lax.dot_general(left_side, right_side, (((1,), (1,)), ((), ())), preferre...  28.8 us
    all_to_all x1, waiting for transfers between devices, body(): lax.all_to_all(send_dy, 'expert', split_axis=0, concat_axis=0, tiled=True)  21.1 us
    gather x1, local copies, waits for them, and re-layouts, body(): outgoing = jnp.take(block_weights, my_units.reshape(-1), axis=1)  21 us
    unnamed x47, local copies, waits for them, and re-layouts  18.5 us
  transfers between devices with their start and end apart: 10, of which 5 were waited for; matrix products, arithmetic and copies ran while one was open for 26% of the time, Pallas kernels for 0%

commit v1 on v0

v1 whole, which is shorter than its diff:
```python
import jax
import jax.numpy as jnp
from jax import lax
from jax.sharding import PartitionSpec as P

F32 = jnp.float32
BF16 = jnp.bfloat16


def silu_parts(preact):
    sigmoid_value = jax.nn.sigmoid(preact)
    return (preact * sigmoid_value, sigmoid_value * (1.0 + preact * (1.0 - sigmoid_value)))


def dot(left, right, left_dim, right_dim):
    return lax.dot_general(
        left, right, (((left_dim,), (right_dim,)), ((), ())), preferred_element_type=F32
    )


def block_ranks(blocks, block):
    width = blocks.shape[-1]
    mask = blocks == block
    upper = lax.broadcasted_iota(jnp.int32, (width, width), 0) < lax.broadcasted_iota(
        jnp.int32, (width, width), 1
    )
    rank = jnp.dot(mask.astype(BF16), upper.astype(BF16), preferred_element_type=F32)
    return mask, rank.astype(jnp.int32)


def body(dense_weights, tokens, cotangent, routes, route_gates, unit_perm, slab_owner):
    n_dp = lax.axis_size("dp")
    n_ex = lax.axis_size("expert")
    row = lax.axis_index("dp")
    col = lax.axis_index("expert")
    _, block_units, feat = dense_weights.shape
    copies, total_units = unit_perm.shape
    slabs = n_ex // copies
    slab_units = total_units // slabs
    share = slab_units // n_dp
    pick = share // n_dp
    tok, width = tokens.shape

    shares = unit_perm.reshape(n_ex, n_dp, share)
    dest = jnp.transpose(shares[slab_owner], (1, 0, 2)).reshape(n_dp * n_ex, share)
    mask, rank = block_ranks(dest // block_units, row)
    place = jnp.where(mask, rank, -1)
    hit = place[:, None, :] == lax.broadcasted_iota(jnp.int32, (1, pick, 1), 1)
    units = jnp.sum(jnp.where(hit, (dest - row * block_units)[:, None, :], 0), axis=2)
    onehot = (
        units.reshape(-1, 1) == lax.broadcasted_iota(jnp.int32, (1, block_units), 1)
    ).astype(BF16)
    picked = dot(onehot, dense_weights, 1, 1).astype(BF16)
    picked = picked.reshape(n_dp * n_ex, pick, 3 * feat)
    arrived = lax.all_to_all(picked, ("dp", "expert"), split_axis=0, concat_axis=0, tiled=True)
    arrived = arrived.reshape(n_dp, n_ex, pick, 3, feat)
    weights = jnp.transpose(arrived, (3, 0, 2, 1, 4)).reshape(3, share, width)
    w_gate, w_up, w_down = weights[0], weights[1], weights[2]

    mine = lax.dynamic_slice(
        shares, (slab_owner[col], row, 0), (1, 1, share)
    ).reshape(1, share)
    mine_block = mine // block_units
    mask, rank = block_ranks(
        jnp.broadcast_to(mine_block, (n_dp, share)),
        lax.broadcasted_iota(jnp.int32, (n_dp, 1), 0),
    )
    at = jnp.sum(
        jnp.where(mask, rank + lax.broadcasted_iota(jnp.int32, (n_dp, 1), 0) * pick, 0), axis=0
    )
    order = (lax.broadcasted_iota(jnp.int32, (share, share), 0) == at[None, :]).astype(BF16)

    part = width // n_dp
    both = jnp.concatenate(
        [
            lax.dynamic_slice(tokens, (0, row * part), (tok, part)),
            lax.dynamic_slice(cotangent, (0, row * part), (tok, part)),
        ],
        axis=1,
    )
    both = lax.all_gather(both, "expert", axis=0, tiled=True)
    both = lax.all_gather(both, "dp", axis=0, tiled=False)
    all_x = jnp.transpose(both[:, :, :part], (1, 0, 2)).reshape(n_ex * tok, width)
    all_c = jnp.transpose(both[:, :, part:], (1, 0, 2)).reshape(n_ex * tok, width)

    gate_table = jnp.sum(
        jnp.where(
            routes[None, :, :] == lax.broadcasted_iota(jnp.int32, (n_ex, 1, 1), 0),
            route_gates[None, :, :],
            0.0,
        ),
        axis=2,
    )
    gate = lax.all_to_all(gate_table, "expert", split_axis=0, concat_axis=0, tiled=True)
    gate = gate.reshape(n_ex * tok, 1)
    copy_id = slab_owner[col] // slabs
    owner_block = lax.broadcasted_iota(jnp.int32, (n_ex, tok), 0).reshape(n_ex * tok, 1)
    both_weight = gate + (owner_block * copies // n_ex == copy_id).astype(F32)

    pre_gate = dot(all_x, w_gate, 1, 1)
    pre_up = dot(all_x, w_up, 1, 1)
    d_hidden = dot(all_c, w_down, 1, 1)
    act, slope = silu_parts(pre_gate)
    hidden = act * pre_up
    d_gate = d_hidden * pre_up * slope
    d_up = d_hidden * act

    out = dot((both_weight * hidden).astype(BF16), w_down, 1, 0).astype(BF16)
    back = (
        dot((both_weight * d_gate).astype(BF16), w_gate, 1, 0)
        + dot((both_weight * d_up).astype(BF16), w_up, 1, 0)
    ).astype(BF16)

    def grad(values, rows):
        ordered = jnp.dot((gate * values).astype(BF16), order, preferred_element_type=F32)
        return dot(ordered.astype(BF16), rows, 0, 0)

    weight_grads = jnp.stack(
        [grad(d_gate, all_x), grad(d_up, all_x), grad(hidden, all_c)]
    ).astype(BF16)[None]

    def collect(partial):
        partial = lax.psum_scatter(partial, "dp", scatter_dimension=1, tiled=True)
        return lax.psum_scatter(partial, "expert", scatter_dimension=0, tiled=True)

    return (collect(out), collect(back), weight_grads)


def solution(mesh):
    in_specs = (
        P(None, "dp", "expert"),
        P("expert", None),
        P("expert", None),
        P("expert", None),
        P("expert", None),
        P(),
        P(),
    )
    out_specs = (P("expert", "dp"), P("expert", "dp"), P("expert", None, "dp", None))
    return jax.shard_map(body, mesh=mesh, in_specs=in_specs, out_specs=out_specs, check_vma=False)
```

time: 811 us -> 504 us (0.62)
  waiting for transfers between devices: 521 us -> 329 us
  local copies, waits for them, and re-layouts: 140 us -> 89.4 us
  other arithmetic: 35.6 us -> 6.16 us
  starting transfers between devices: 26.8 us -> 10.2 us
  matrix products: 63.6 us -> 49.6 us
    all_gather x1 -> x2, waiting for transfers between devices: 430 us -> 53.3 us  [the longest x1 53.3 us: body(): both = lax.all_gather(both, 'expert', axis=0, tiled=True)]
    reduce_scatter x4, waiting for transfers between devices: 0.04 us -> 181 us  [the longest x2 112 us: collect(): return lax.psum_scatter(partial, 'expert', scatter_dimension=0, tiled=True)]
    gather x10 -> x1, local copies, waits for them, and re-layouts: 64.2 us -> 0.58 us  [body(): shares[slab_owner]]
    slice x3 -> x4, local copies, waits for them, and re-layouts: 49.5 us -> 14.1 us  [body(): w_gate, w_up, w_down = (weights[0], weights[1], weights[2])]
    convert_element_type x0 -> x1, local copies, waits for them, and re-layouts: none -> 23.3 us  [body(): picked = dot(onehot, dense_weights, 1, 1).astype(BF16)]
    reshape x4 -> x3, local copies, waits for them, and re-layouts: 2.82 us -> 25 us  [the longest x1 12.5 us: body(): picked = picked.reshape(n_dp * n_ex, pick, 3 * feat)]
    transpose x0 -> x3, local copies, waits for them, and re-layouts: none -> 18.8 us  [the longest x2 12.5 us: body(): jnp.transpose(both[:, :, part:], (1, 0, 2)).reshape(n_ex * tok, width)]
    all_to_all x5 -> x2, starting transfers between devices: 26.1 us -> 9.33 us  [the longest x1 6.02 us: body(): lax.all_to_all(picked, ('dp', 'expert'), split_axis=0, concat_axis=0, til...]
  transfers between devices with their start and end apart: 10 -> 8, of which waited for: 5 -> 6; matrix products, arithmetic and copies ran while one was open for 26% -> 24% of each run, Pallas kernels for 0% -> 0%
where the time goes in v1:
time: 504 us; the launch traced here: 503 us
  waiting for transfers between devices  329 us (65%)
  local copies, waits for them, and re-layouts  89.4 us (18%)
  matrix products  49.6 us (10%)
  between operations  18.3 us (4%)
  starting transfers between devices  10.2 us (2%)
  other arithmetic  6.16 us (1%)
    reduce_scatter x2, waiting for transfers between devices, collect(): return lax.psum_scatter(partial, 'expert', scatter_dimension=0, tiled=True)  112 us
    all_to_all x1, waiting for transfers between devices, body(): lax.all_to_all(picked, ('dp', 'expert'), split_axis=0, concat_axis=0, til...  95.2 us
    reduce_scatter x2, waiting for transfers between devices, collect(): partial = lax.psum_scatter(partial, 'dp', scatter_dimension=1, tiled=True)  68.3 us
    all_gather x1, waiting for transfers between devices, body(): both = lax.all_gather(both, 'expert', axis=0, tiled=True)  53.3 us
    dot_general x10, matrix products, dot(): lax.dot_general(left, right, (((left_dim,), (right_dim,)), ((), ())), pre...  49.2 us
    convert_element_type x1, local copies, waits for them, and re-layouts, body(): picked = dot(onehot, dense_weights, 1, 1).astype(BF16)  23.3 us
    slice x4, local copies, waits for them, and re-layouts, body(): w_gate, w_up, w_down = (weights[0], weights[1], weights[2])  14.1 us
    transpose x2, local copies, waits for them, and re-layouts, body(): jnp.transpose(both[:, :, part:], (1, 0, 2)).reshape(n_ex * tok, width)  12.5 us
  transfers between devices with their start and end apart: 8, of which 6 were waited for; matrix products, arithmetic and copies ran while one was open for 24% of the time, Pallas kernels for 0%

profile of v1, /device:TPU:0, one launch (start us, length us, event | category | flops | bytes accessed | tf_op | source)
XLA Modules:
  0.0 503.0 jit_solution(6462021261323485056)
XLA Ops:
  7.2 1.1 constant_dynamic-slice_fusion.1
  8.4 0.7 pad_maximum_fusion.1
  9.2 53.3 %all-gather.4.cloned.1.call-done = bf16[1024,1024]{1,0:T(8,128)(2,1)} async-done(((bf16[128,1024]{1,0:T(8,128)(2,1)}), bf16[1024,1024]{1,0:T(8,128)(2,1)}) %all-gather.4.cloned.1.call-update) | async-done | bytes 2097168 | tf_op jit(solution)/shard_map/all_gather | solution.py:81
  62.6 0.6 select_reduce_fusion.1
  63.2 3.3 all-to-all-start
  66.5 0.1 reshape.211
  66.7 0.6 gather_fusion
  67.3 0.1 fusion.42
  67.4 0.2 fusion.11
  67.6 0.6 select_reduce_fusion
  68.2 0.1 eq.84
  68.3 8.0 %fusion.4 = bf16[2816,3,256]{2,0,1:T(8,128)(2,1)S(1)} fusion(bf16[3,1408,256]{2,1,0:T(8,128)(2,1)S(1)} %copy-done, s32[2816]{0:T(1024)S(1)} %eq.84), kind=kOutput, calls=%fused_computation.6 | convolution fusion | flops 6096257024 | bytes 6499328 | tf_op jit(solution)/shard_map/dot_general | solution.py:16
  76.3 23.3 %copy.47 = bf16[2816,3,256]{2,1,0:T(4,128)(2,1)} copy(bf16[2816,3,256]{2,0,1:T(8,128)(2,1)S(1)} %fusion.4) | data formatting | bytes 8650752 | tf_op jit(solution)/shard_map/convert_element_type | solution.py:53
  99.5 12.5 %reshape.212 = bf16[32,88,768]{2,1,0:T(8,128)(2,1)} reshape(bf16[2816,3,256]{2,1,0:T(4,128)(2,1)} %copy.47) | data formatting | bytes 8650752 | tf_op jit(solution)/shard_map/reshape | solution.py:54
  112.0 6.0 %all-to-all-start.1 = ((bf16[32,88,768]{2,1,0:T(8,128)(2,1)}), bf16[32,88,768]{2,1,0:T(8,128)(2,1)}, u32[]{:S(2)}, u32[]{:S(2)}) async-start(bf16[32,88,768]{2,1,0:T(8,128)(2,1)} %reshape.212), calls=%async_computation.1 | async-start | bytes 8650752 | tf_op jit(solution)/shard_map/all_to_all | solution.py:55
  118.0 0.2 reduce-scatter.5.cloned.1.call-start
  118.3 0.6 dynamic_slice.13
  121.5 95.2 %all-to-all-done.1 = bf16[32,88,768]{2,1,0:T(8,128)(2,1)} async-done(((bf16[32,88,768]{2,1,0:T(8,128)(2,1)}), bf16[32,88,768]{2,1,0:T(8,128)(2,1)}, u32[]{:S(2)}, u32[]{:S(2)}) %all-to-all-start.1) | async-done | bytes 4325408 | tf_op jit(solution)/shard_map/all_to_all | solution.py:55
  216.7 12.4 %reshape.213 = bf16[4,8,88,3,256]{4,3,2,1,0:T(4,128)(2,1)} reshape(bf16[32,88,768]{2,1,0:T(8,128)(2,1)} %all-to-all-done.1) | data formatting | bytes 8650752 | tf_op jit(solution)/shard_map/reshape | solution.py:56
  229.0 11.6 %fusion.57 = (bf16[1,4,88,8,256]{4,0,2,3,1:T(2,128)(2,1)S(1)}, bf16[1,4,88,8,256]{4,0,2,3,1:T(2,128)(2,1)S(1)}, bf16[1,4,88,8,256]{4,0,2,3,1:T(2,128)(2,1)S(1)}) fusion(bf16[3,4,88,8,256]{4,0,2,3,1:T(4,128)(2,1)} %bitcast.88), kind=kLoop, calls=%fused_computation.93 | loop fusion | bytes 8650752 | tf_op jit(solution)/shard_map/slice | solution.py:58
  240.6 0.8 copy.48
  241.5 1.5 copy.52
  243.0 0.8 copy.50
  243.8 1.6 copy.54
  245.4 0.8 copy.49
  246.3 1.5 copy.53
  247.8 5.9 %slice_bitcast_fusion = (bf16[1024,4,512]{2,0,1:T(8,128)(2,1)}, bf16[1024,4,512]{2,0,1:T(8,128)(2,1)}) fusion(bf16[4,1024,1024]{2,1,0:T(8,128)(2,1)} %bitcast.89), kind=kLoop, calls=%fused_computation.10 | loop fusion | bytes 16777216 | tf_op jit(solution)/shard_map/transpose | solution.py:84
  253.7 6.3 %copy.43 = bf16[1024,4,512]{0,2,1:T(8,128)(2,1)} copy(bf16[1024,4,512]{2,0,1:T(8,128)(2,1)} %get-tuple-element.4) | data formatting | bytes 8388608 | tf_op jit(solution)/shard_map/transpose | solution.py:83
  259.9 4.4 fusion.58
  264.4 1.7 fusion.59
  266.1 1.1 copy-done.7
  267.2 4.4 convolution_convert_fusion
  271.7 0.3 reduce-scatter.9.cloned.1.call-start
  271.9 6.7 %copy.51 = bf16[1024,4,512]{0,2,1:T(8,128)(2,1)} copy(bf16[1024,4,512]{2,0,1:T(8,128)(2,1)} %get-tuple-element.3) | data formatting | bytes 8388608 | tf_op jit(solution)/shard_map/transpose | solution.py:84
  278.6 4.7 fusion.60
  283.3 2.8 fusion.15
  286.1 4.7 add_convert_fusion
  290.9 0.0 reduce-scatter.7.cloned.1.call-start
  290.9 22.8 %reduce-scatter.5.cloned.1.call-done = bf16[1024,512]{1,0:T(8,128)(2,1)} async-done(((bf16[1024,2048]{1,0:T(8,128)(2,1)}), bf16[1024,512]{1,0:T(8,128)(2,1)}) %reduce-scatter.5.cloned.1.call-update) | async-done | bytes 1048592 | tf_op jit(solution)/shard_map/reduce_scatter | solution.py:123
  313.8 0.3 reduce-scatter.11.cloned.1.call-start
  315.5 0.2 fusion.14
  315.6 45.5 %reduce-scatter.9.cloned.1.call-done = bf16[1024,512]{1,0:T(8,128)(2,1)} async-done(((bf16[1024,2048]{1,0:T(8,128)(2,1)}), bf16[1024,512]{1,0:T(8,128)(2,1)}) %reduce-scatter.9.cloned.1.call-update) | async-done | bytes 1048592 | tf_op jit(solution)/shard_map/reduce_scatter | solution.py:123
  361.1 6.1 %fusion.8 = bf16[1,1,352,2048]{3,2,1,0:T(8,128)(2,1)} fusion(bf16[1024,2048]{0,1:T(8,128)(2,1)} %bitcast.98, f32[1024]{0:T(1024)S(1)} %bitcast.107, f32[1024,352]{0,1:T(8,128)} %copy-done.2, s32[352]{0:T(512)S(1)} %fusion.14, f32[1024,352]{0,1:T(8,128)S(1)} %fusion.58), kind=kOutput, calls=%fused_computation.17 | convolution fusion | flops 1733878784 | bytes 8525184 | tf_op jit(solution)/shard_map/dot_general | solution.py:16
  367.2 6.0 %fusion.9 = bf16[1,1,352,2048]{3,2,1,0:T(8,128)(2,1)} fusion(bf16[1024,2048]{0,1:T(8,128)(2,1)} %bitcast.102, f32[1024]{0:T(1024)S(1)} %bitcast.108, f32[1024,352]{0,1:T(8,128)} %copy-done.7, s32[352]{0:T(512)S(1)} %fusion.14, f32[1024,352]{0,1:T(8,128)S(1)} %fusion.58), kind=kOutput, calls=%fused_computation.18 | convolution fusion | flops 1733878784 | bytes 8525184 | tf_op jit(solution)/shard_map/dot_general | solution.py:16
  373.2 6.5 %fusion.7 = bf16[1,1,352,2048]{3,2,1,0:T(8,128)(2,1)} fusion(bf16[1024,2048]{0,1:T(8,128)(2,1)} %bitcast.99, f32[1024]{0:T(1024)S(1)} %bitcast.109, s32[352]{0:T(512)S(1)} %fusion.14, f32[1024,352]{0,1:T(8,128)S(1)} %fusion.58, f32[1024,352]{0,1:T(8,128)} %copy-done.2, f32[1024,352]{0,1:T(8,128)} %copy-done.7), kind=kOutput, calls=%fused_computation.16 | convolution fusion | flops 1735320576 | bytes 9966976 | tf_op jit(solution)/shard_map/dot_general | solution.py:16
  379.7 4.0 pad_maximum_fusion
  383.7 45.4 %reduce-scatter.7.cloned.1.call-done = bf16[128,512]{1,0:T(8,128)(2,1)} async-done(((bf16[1024,512]{1,0:T(8,128)(2,1)}), bf16[128,512]{1,0:T(8,128)(2,1)}) %reduce-scatter.7.cloned.1.call-update) | async-done | bytes 131088 | tf_op jit(solution)/shard_map/reduce_scatter | solution.py:124
  429.1 67.0 %reduce-scatter.11.cloned.1.call-done = bf16[128,512]{1,0:T(8,128)(2,1)} async-done(((bf16[1024,512]{1,0:T(8,128)(2,1)}), bf16[128,512]{1,0:T(8,128)(2,1)}) %reduce-scatter.11.cloned.1.call-update) | async-done | bytes 131088 | tf_op jit(solution)/shard_map/reduce_scatter | solution.py:124
  (46 shorter events, 0.4 us)
Async XLA Ops:
  7.2 61.1 %copy-start = (bf16[3,1408,256]{2,1,0:T(8,128)(2,1)S(1)}, bf16[3,1408,256]{2,1,0:T(8,128)(2,1)}, u32[]{:S(2)}) copy-start(bf16[3,1408,256]{2,1,0:T(8,128)(2,1)} %param.7) | copy-start | bytes 6488068
  7.2 55.3 %all-gather.4.cloned.1.call-start = ((), (), s32[]{:S(2)}) async-start(), calls=%async_computation.6 | async-start | bytes 2359296 | tf_op jit(solution)/shard_map/all_gather | solution.py:81
  8.4 54.2 %copy-start.11 = (f32[128,4]{0,1:T(4,128)S(1)}, f32[128,4]{0,1:T(4,128)}, u32[]{:S(2)}) copy-start(f32[128,4]{0,1:T(4,128)} %param.11) | copy-start | bytes 6148
  8.4 54.2 %copy-start.12 = (s32[128,4]{0,1:T(4,128)S(1)}, s32[128,4]{0,1:T(4,128)}, u32[]{:S(2)}) copy-start(s32[128,4]{0,1:T(4,128)} %param.10) | copy-start | bytes 6148
  8.4 58.1 %copy-start.10 = (s32[2,5632]{1,0:T(2,128)S(1)}, s32[2,5632]{1,0:T(2,128)}, u32[]{:S(2)}) copy-start(s32[2,5632]{1,0:T(2,128)} %param.12) | copy-start | bytes 135172
  8.4 58.2 %copy-start.13 = (s32[8]{0:T(128)S(1)}, s32[8]{0:T(128)}, u32[]{:S(2)}) copy-start(s32[8]{0:T(128)} %param.13) | copy-start | bytes 100
  9.2 238.6 %all-gather.6.cloned.1.call-start = ((), (), s32[]{:S(2)}) async-start(), calls=%async_computation.11 | async-start | bytes 10485760 | tf_op jit(solution)/shard_map/all_gather | solution.py:82
  63.2 48.8 %all-to-all-start = ((f32[8,1,128]{2,1,0:T(1,128)}), f32[8,1,128]{2,1,0:T(1,128)S(1)}, u32[]{:S(2)}, u32[]{:S(2)}) async-start(f32[8,1,128]{2,1,0:T(1,128)} %bitcast.1), calls=%async_computation | async-start | bytes 8192 | tf_op jit(solution)/shard_map/all_to_all | solution.py:94
  112.0 104.7 %all-to-all-start.1 = ((bf16[32,88,768]{2,1,0:T(8,128)(2,1)}), bf16[32,88,768]{2,1,0:T(8,128)(2,1)}, u32[]{:S(2)}, u32[]{:S(2)}) async-start(bf16[32,88,768]{2,1,0:T(8,128)(2,1)} %reshape.212), calls=%async_computation.1 | async-start | bytes 8650752 | tf_op jit(solution)/shard_map/all_to_all | solution.py:55
  118.0 195.7 %reduce-scatter.5.cloned.1.call-start = ((), (), s32[]{:S(2)}) async-start(), calls=%async_computation.7 | async-start | bytes 5242880 | tf_op jit(solution)/shard_map/reduce_scatter | solution.py:123
  259.9 4.4 copy-start.4
  259.9 4.4 copy-start.6
  264.4 2.8 copy-start.9
  266.1 1.1 copy-start.7
  271.7 89.5 %reduce-scatter.9.cloned.1.call-start = ((), (), s32[]{:S(2)}) async-start(), calls=%async_computation.9 | async-start | bytes 5242880 | tf_op jit(solution)/shard_map/reduce_scatter | solution.py:123
  278.6 4.7 copy-start.3
  278.6 4.7 copy-start.8
  283.3 2.8 copy-start.2
  283.3 2.8 copy-start.5
  290.9 138.3 %reduce-scatter.7.cloned.1.call-start = ((), (), s32[]{:S(2)}) async-start(), calls=%async_computation.8 | async-start | bytes 1179648 | tf_op jit(solution)/shard_map/reduce_scatter | solution.py:124
  313.8 182.4 %reduce-scatter.11.cloned.1.call-start = ((), (), s32[]{:S(2)}) async-start(), calls=%async_computation.10 | async-start | bytes 1179648 | tf_op jit(solution)/shard_map/reduce_scatter | solution.py:124
  379.7 116.4 %copy-start.1 = (bf16[3,1408,256]{2,1,0:T(8,128)(2,1)S(1)}, bf16[3,1408,256]{2,1,0:T(8,128)(2,1)}, u32[]{:S(2)}) copy-start(bf16[3,1408,256]{2,1,0:T(8,128)(2,1)} %param.7) | copy-start | bytes 6488068
Sparse Core Ops, SparseCore 0:
  10.7 51.7 all-gather.3
  64.1 56.8 all-gather.5
  271.8 41.9 reduce-scatter.4
  316.7 44.3 reduce-scatter.8
  364.9 64.1 reduce-scatter.6
  433.0 63.1 reduce-scatter.10

commit v2 on v1

--- a/solution.py
+++ b/solution.py
@@ -1,6 +1,10 @@
+import functools
+
 import jax
 import jax.numpy as jnp
 from jax import lax
+from jax.experimental import pallas as pl
+from jax.experimental.pallas import tpu as pltpu
 from jax.sharding import PartitionSpec as P
 
 F32 = jnp.float32
@@ -26,6 +30,172 @@
     )
     rank = jnp.dot(mask.astype(BF16), upper.astype(BF16), preferred_element_type=F32)
     return mask, rank.astype(jnp.int32)
+
+
+def log2(count):
+    return count.bit_length() - 1
+
+
+def flip(index, place):
+    return index + (1 - 2 * (index // (1 << place) % 2)) * (1 << place)
+
+
+def peer(device, n_ex):
+    return {"dp": device // n_ex, "expert": device % n_ex}
+
+
+STREAMS = 4
+
+
+def halving_orders(dp_bits, ex_bits):
+    rest = [ex_bits + bit for bit in range(1, dp_bits)] + list(range(ex_bits))
+    turns = [[0, 1, 2], [1, 2, 0], [2, 0, 1], [1, 0, 2]]
+    orders = []
+    for turn in turns:
+        head = [rest[at] for at in turn if at < len(rest)]
+        orders.append([ex_bits] + head + rest[len(head) :])
+    return orders
+
+
+def halving_kernel(n_dp, n_ex, n_arrays, *refs):
+    ins, outs = refs[:n_arrays], refs[n_arrays : 2 * n_arrays]
+    data, recv, load_sem, send_sem, recv_sem = refs[2 * n_arrays :]
+    me = lax.axis_index("dp") * n_ex + lax.axis_index("expert")
+    bits = log2(n_dp) + log2(n_ex)
+    orders = halving_orders(log2(n_dp), log2(n_ex))
+    rows, part = data.shape[2:]
+    splits = STREAMS // n_arrays
+
+    for stream in range(STREAMS):
+        source, at = ins[stream // splits], stream % splits
+        for g in range(n_dp):
+
+            def load(e, carry, source=source, at=at, g=g, stream=stream):
+                start = pl.multiple_of(e * (rows * splits) + at * rows, rows)
+                pltpu.make_async_copy(
+                    source.at[pl.ds(start, rows), pl.ds(g * part, part)],
+                    data.at[stream, g * n_ex + e],
+                    load_sem.at[stream],
+                ).start()
+                return carry
+
+            lax.fori_loop(0, n_ex, load, 0)
+
+    barrier = pltpu.get_barrier_semaphore()
+    for place in range(bits):
+        pl.semaphore_signal(
+            barrier,
+            inc=1,
+            device_id=peer(flip(me, place), n_ex),
+            device_id_type=pl.DeviceIdType.MESH,
+        )
+    pl.semaphore_wait(barrier, bits)
+
+    def block_of(stream, step, choice, sent):
+        order = orders[stream]
+        index = 0
+        for place in order[: step + 1]:
+            index = index + me // (1 << place) % 2 * (1 << place)
+        if sent:
+            index = flip(index, order[step])
+        for bit, place in enumerate(sorted(order[step + 1 :])):
+            index = index + choice // (1 << bit) % 2 * (1 << place)
+        return index
+
+    def count(step):
+        return 1 << (bits - 1 - step)
+
+    def offset(step):
+        return (1 << bits) - (1 << (bits - step))
+
+    def send(stream, step, choice):
+        pltpu.make_async_remote_copy(
+            src_ref=data.at[stream, block_of(stream, step, choice, True)],
+            dst_ref=recv.at[stream, offset(step) + choice],
+            send_sem=send_sem.at[stream, step],
+            recv_sem=recv_sem.at[stream, step],
+            device_id=peer(flip(me, orders[stream][step]), n_ex),
+            device_id_type=pl.DeviceIdType.MESH,
+        ).start()
+
+    def region(stream, step):
+        view = recv.at[stream, pl.ds(offset(step), count(step))]
+        return pltpu.make_async_remote_copy(
+            src_ref=view,
+            dst_ref=view,
+            send_sem=send_sem.at[stream, step],
+            recv_sem=recv_sem.at[stream, step],
+            device_id=peer(flip(me, orders[stream][step]), n_ex),
+            device_id_type=pl.DeviceIdType.MESH,
+        )
+
+    def number(stream, step, choice, sent):
+        order = orders[stream]
+        later = sorted(order[step + 1 :])
+        place = order[step + 1]
+        mine = me // (1 << place) % 2
+        value = (1 - mine if sent else mine) * (1 << later.index(place))
+        for bit, other in enumerate(sorted(order[step + 2 :])):
+            value = value + choice // (1 << bit) % 2 * (1 << later.index(other))
+        return value
+
+    for stream in range(STREAMS):
+        pltpu.make_async_copy(data.at[stream], data.at[stream], load_sem.at[stream]).wait()
+
+        def first(choice, carry, stream=stream):
+            send(stream, 0, choice)
+            return carry
+
+        lax.fori_loop(0, count(0), first, 0)
+
+    for step in range(bits):
+        for stream in range(STREAMS):
+            region(stream, step).wait_recv()
+            if step == bits - 1:
+                total = data[stream, me].astype(F32) + recv[stream, offset(step)].astype(F32)
+                outs[stream // splits][pl.ds(stream % splits * rows, rows), :] = total.astype(BF16)
+                continue
+            for sent in (True, False):
+
+                def add(choice, carry, stream=stream, step=step, sent=sent):
+                    block = block_of(stream, step + 1, choice, sent)
+                    slot = offset(step) + number(stream, step, choice, sent)
+                    total = data[stream, block].astype(F32) + recv[stream, slot].astype(F32)
+                    data[stream, block] = total.astype(BF16)
+                    if sent:
+                        send(stream, step + 1, choice)
+                    return carry
+
+                lax.fori_loop(0, count(step + 1), add, 0)
+
+    for step in range(bits):
+        for stream in range(STREAMS):
+            region(stream, step).wait_send()
+
+
+def halving_sum(n_dp, n_ex, arrays):
+    total, width = arrays[0].shape
+    tok, part, n_arrays = total // n_ex, width // n_dp, len(arrays)
+    rows = tok * n_arrays // STREAMS
+    blocks = n_dp * n_ex
+    steps = log2(blocks)
+    return pl.pallas_call(
+        functools.partial(halving_kernel, n_dp, n_ex, n_arrays),
+        out_shape=[jax.ShapeDtypeStruct((tok, part), BF16)] * n_arrays,
+        in_specs=[pl.BlockSpec(memory_space=pl.ANY)] * n_arrays,
+        out_specs=[pl.BlockSpec(memory_space=pltpu.VMEM)] * n_arrays,
+        scratch_shapes=[
+            pltpu.VMEM((STREAMS, blocks, rows, part), BF16),
+            pltpu.VMEM((STREAMS, blocks - 1, rows, part), BF16),
+            pltpu.SemaphoreType.DMA((STREAMS,)),
+            pltpu.SemaphoreType.DMA((STREAMS, steps)),
+            pltpu.SemaphoreType.DMA((STREAMS, steps)),
+        ],
+        compiler_params=pltpu.CompilerParams(
+            collective_id=1, has_side_effects=True, vmem_limit_bytes=60 << 20
+        ),
+        name="halving_sum",
+    )(*arrays)
 
 
 def body(dense_weights, tokens, cotangent, routes, route_gates, unit_perm, slab_owner):
@@ -50,7 +220,8 @@
     onehot = (
         units.reshape(-1, 1) == lax.broadcasted_iota(jnp.int32, (1, block_units), 1)
     ).astype(BF16)
-    picked = dot(onehot, dense_weights, 1, 1).astype(BF16)
+    side = jnp.concatenate([dense_weights[0], dense_weights[1], dense_weights[2]], axis=1)
+    picked = dot(onehot, side, 1, 0).astype(BF16)
     picked = picked.reshape(n_dp * n_ex, pick, 3 * feat)
     arrived = lax.all_to_all(picked, ("dp", "expert"), split_axis=0, concat_axis=0, tiled=True)
     arrived = arrived.reshape(n_dp, n_ex, pick, 3, feat)
@@ -119,11 +290,12 @@
         [grad(d_gate, all_x), grad(d_up, all_x), grad(hidden, all_c)]
     ).astype(BF16)[None]
 
-    def collect(partial):
-        partial = lax.psum_scatter(partial, "dp", scatter_dimension=1, tiled=True)
-        return lax.psum_scatter(partial, "expert", scatter_dimension=0, tiled=True)
-
-    return (collect(out), collect(back), weight_grads)
+    if out.size * out.dtype.itemsize <= 1 << 23:
+        mixed, token_grad = halving_sum(n_dp, n_ex, [out, back])
+    else:
+        (mixed,) = halving_sum(n_dp, n_ex, [out])
+        (token_grad,) = halving_sum(n_dp, n_ex, [back])
+    return (mixed, token_grad, weight_grads)
 
 
 def solution(mesh):

time: 504 us -> 336 us (0.67)
  waiting for transfers between devices: 329 us -> 137 us
  Pallas kernels: 0 us -> 54.7 us
  local copies, waits for them, and re-layouts: 89.4 us -> 53.9 us
    reduce_scatter x4 -> x0, waiting for transfers between devices: 181 us -> none  [the longest x2 112 us: collect(): return lax.psum_scatter(partial, 'expert', scatter_dimension=0, tiled=True)]
    pallas_call x0 -> x1, Pallas kernels: none -> 54.7 us  [halving_sum(): pl.pallas_call(functools.partial(halving_kernel, n_dp, n_ex, n_arrays), o...]
    convert_element_type x1 -> x0, local copies, waits for them, and re-layouts: 23.3 us -> none  [body(): picked = dot(onehot, dense_weights, 1, 1).astype(BF16)]
    reshape x1 -> x0, local copies, waits for them, and re-layouts: 12.5 us -> none  [body(): picked = picked.reshape(n_dp * n_ex, pick, 3 * feat)]
    all_gather x1, waiting for transfers between devices: 53.3 us -> 43.4 us  [body(): both = lax.all_gather(both, 'expert', axis=0, tiled=True)]
  transfers between devices with their start and end apart: 8 -> 4, of which waited for: 6 -> 2; matrix products, arithmetic and copies ran while one was open for 24% -> 13% of each run, Pallas kernels for 0% -> 0%
where the time goes in v2:
time: 336 us; the launch traced here: 334 us
  waiting for transfers between devices  137 us (41%)
  Pallas kernels  54.7 us (16%)
  local copies, waits for them, and re-layouts  53.9 us (16%)
  matrix products  53.1 us (16%)
  between operations  18.2 us (5%)
  starting transfers between devices  11.1 us (3%)
  other arithmetic  6.31 us (2%)
    all_to_all x1, waiting for transfers between devices, body(): lax.all_to_all(picked, ('dp', 'expert'), split_axis=0, concat_axis=0, til...  93.7 us
    pallas_call x1, Pallas kernels, halving_sum(): pl.pallas_call(functools.partial(halving_kernel, n_dp, n_ex, n_arrays), o...  54.7 us
    dot_general x10, matrix products, dot(): lax.dot_general(left, right, (((left_dim,), (right_dim,)), ((), ())), pre...  52.8 us
    all_gather x1, waiting for transfers between devices, body(): both = lax.all_gather(both, 'expert', axis=0, tiled=True)  43.4 us
    slice x4, local copies, waits for them, and re-layouts, body(): w_gate, w_up, w_down = (weights[0], weights[1], weights[2])  14.4 us
    reshape x1, local copies, waits for them, and re-layouts, body(): arrived = arrived.reshape(n_dp, n_ex, pick, 3, feat)  12.4 us
    transpose x2, local copies, waits for them, and re-layouts, body(): jnp.transpose(both[:, :, part:], (1, 0, 2)).reshape(n_ex * tok, width)  12.1 us
    all_to_all x1, starting transfers between devices, body(): lax.all_to_all(gate_table, 'expert', split_axis=0, concat_axis=0, tiled=T...  7.31 us
  transfers between devices with their start and end apart: 4, of which 2 were waited for; matrix products, arithmetic and copies ran while one was open for 13% of the time, Pallas kernels for 0%

profile of v2, /device:TPU:0, one launch (start us, length us, event | category | flops | bytes accessed | tf_op | source)
XLA Modules:
  0.0 334.5 jit_solution(16071971062717883023)
XLA Ops:
  7.2 0.0 all-gather.4.cloned.1.call-start
  7.2 1.0 constant_dynamic-slice_fusion.1
  8.2 0.7 pad_maximum_fusion.1
  9.0 0.0 all-gather.4.cloned.1.call-update
  9.0 1.3 select_reduce_fusion.1
  10.3 7.3 %all-to-all-start = ((f32[8,1,128]{2,1,0:T(1,128)}), f32[8,1,128]{2,1,0:T(1,128)S(1)}, u32[]{:S(2)}, u32[]{:S(2)}) async-start(f32[8,1,128]{2,1,0:T(1,128)} %bitcast.1), calls=%async_computation | async-start | bytes 8192 | tf_op jit(solution)/shard_map/all_to_all | solution.py:265
  17.6 0.0 all-gather.6.cloned.1.call-start
  17.6 0.9 reshape.211
  18.5 0.0 copy-done.10
  18.6 0.6 gather_fusion
  19.2 43.4 %all-gather.4.cloned.1.call-done = bf16[1024,1024]{1,0:T(8,128)(2,1)} async-done(((bf16[128,1024]{1,0:T(8,128)(2,1)}), bf16[1024,1024]{1,0:T(8,128)(2,1)}) %all-gather.4.cloned.1.call-update) | async-done | bytes 2097168 | tf_op jit(solution)/shard_map/all_gather | solution.py:252
  62.5 0.0 all-gather.6.cloned.1.call-update
  62.6 0.1 fusion.43
  62.7 0.2 fusion.12
  62.9 0.6 select_reduce_fusion
  63.5 0.1 eq.84
  63.6 0.6 copy-done.4
  64.1 0.1 slice_bitcast_fusion.4
  64.3 9.4 %fusion.2 = bf16[2816,768]{1,0:T(8,128)(2,1)} fusion(s32[2816]{0:T(1024)S(1)} %eq.84, bf16[1408,256]{1,0:T(8,128)(2,1)S(1)} %get-tuple-element.13, bf16[1408,256]{1,0:T(8,128)(2,1)S(1)} %get-tuple-element.14, bf16[1408,256]{1,0:T(8,128)(2,1)S(1)} %get-tuple-element.12), kind=kOutput, calls=%fused_computation.5 | convolution fusion | flops 6102745088 | bytes 6499328 | tf_op jit(solution)/shard_map/dot_general | solution.py:20
  73.7 0.0 all-to-all-done
  73.7 3.8 %all-to-all-start.1 = ((bf16[32,88,768]{2,1,0:T(8,128)(2,1)}), bf16[32,88,768]{2,1,0:T(8,128)(2,1)}, u32[]{:S(2)}, u32[]{:S(2)}) async-start(bf16[32,88,768]{2,1,0:T(8,128)(2,1)} %bitcast.98), calls=%async_computation.1 | async-start | bytes 8650752 | tf_op jit(solution)/shard_map/all_to_all | solution.py:226
  77.4 0.6 dynamic_slice.13
  82.0 0.2 fusion.15
  82.2 93.7 %all-to-all-done.1 = bf16[32,88,768]{2,1,0:T(8,128)(2,1)} async-done(((bf16[32,88,768]{2,1,0:T(8,128)(2,1)}), bf16[32,88,768]{2,1,0:T(8,128)(2,1)}, u32[]{:S(2)}, u32[]{:S(2)}) %all-to-all-start.1) | async-done | bytes 4325408 | tf_op jit(solution)/shard_map/all_to_all | solution.py:226
  175.9 12.4 %reshape.213 = bf16[4,8,88,3,256]{4,3,2,1,0:T(4,128)(2,1)} reshape(bf16[32,88,768]{2,1,0:T(8,128)(2,1)} %all-to-all-done.1) | data formatting | bytes 8650752 | tf_op jit(solution)/shard_map/reshape | solution.py:227
  188.3 11.9 %fusion.59 = (bf16[1,4,88,8,256]{4,0,2,3,1:T(2,128)(2,1)S(1)}, bf16[1,4,88,8,256]{4,0,2,3,1:T(2,128)(2,1)S(1)}, bf16[1,4,88,8,256]{4,0,2,3,1:T(2,128)(2,1)S(1)}) fusion(bf16[3,4,88,8,256]{4,0,2,3,1:T(4,128)(2,1)} %bitcast.89), kind=kLoop, calls=%fused_computation.101 | loop fusion | bytes 8650752 | tf_op jit(solution)/shard_map/slice | solution.py:229
  200.1 0.8 copy.44
  201.0 1.5 copy.48
  202.5 0.8 copy.45
  203.4 0.4 copy.49
  203.8 0.8 copy.46
  204.7 1.5 copy.50
  206.2 5.8 %slice_bitcast_fusion = (bf16[1024,4,512]{2,0,1:T(8,128)(2,1)}, bf16[1024,4,512]{2,0,1:T(8,128)(2,1)}) fusion(bf16[4,1024,1024]{2,1,0:T(8,128)(2,1)} %bitcast.90), kind=kLoop, calls=%fused_computation.9 | loop fusion | bytes 16777216 | tf_op jit(solution)/shard_map/transpose | solution.py:255
  212.1 6.3 %copy.40 = bf16[1024,4,512]{0,2,1:T(8,128)(2,1)} copy(bf16[1024,4,512]{2,0,1:T(8,128)(2,1)} %get-tuple-element.8) | data formatting | bytes 8388608 | tf_op jit(solution)/shard_map/transpose | solution.py:254
  218.4 4.4 %fusion.60 = f32[1024,352]{0,1:T(8,128)S(1)} fusion(bf16[352,2048]{1,0:T(8,128)(2,1)} %bitcast.96, bf16[1024,2048]{0,1:T(8,128)(2,1)} %bitcast.99), kind=kOutput, calls=%fused_computation.102 | convolution fusion | flops 1476395008 | bytes 7077888 | tf_op jit(solution)/shard_map/dot_general | solution.py:20
  222.8 2.8 fusion.61
  225.6 6.3 %copy.47 = bf16[1024,4,512]{0,2,1:T(8,128)(2,1)} copy(bf16[1024,4,512]{2,0,1:T(8,128)(2,1)} %get-tuple-element.7) | data formatting | bytes 8388608 | tf_op jit(solution)/shard_map/transpose | solution.py:255
  231.9 4.3 %fusion.62 = f32[1024,352]{0,1:T(8,128)S(1)} fusion(bf16[352,2048]{1,0:T(8,128)(2,1)} %bitcast.105, bf16[1024,2048]{0,1:T(8,128)(2,1)} %bitcast.103), kind=kOutput, calls=%fused_computation.104 | convolution fusion | flops 1476395008 | bytes 7077888 | tf_op jit(solution)/shard_map/dot_general | solution.py:20
  236.2 5.6 %fusion.4 = bf16[1,1,352,2048]{3,2,1,0:T(8,128)(2,1)} fusion(bf16[1024,2048]{0,1:T(8,128)(2,1)} %bitcast.100, f32[1024]{0:T(1024)S(1)} %bitcast.109, f32[1024,352]{0,1:T(8,128)S(1)} %fusion.62, s32[352]{0:T(512)S(1)} %fusion.15, f32[1024,352]{0,1:T(8,128)S(1)} %fusion.60), kind=kOutput, calls=%fused_computation.16 | convolution fusion | flops 1733878784 | bytes 8525184 | tf_op jit(solution)/shard_map/dot_general | solution.py:20
  241.8 6.1 %fusion.3 = bf16[1,1,352,2048]{3,2,1,0:T(8,128)(2,1)} fusion(bf16[1024,2048]{0,1:T(8,128)(2,1)} %bitcast.101, f32[1024]{0:T(1024)S(1)} %bitcast.110, s32[352]{0:T(512)S(1)} %fusion.15, f32[1024,352]{0,1:T(8,128)S(1)} %fusion.60, f32[1024,352]{0,1:T(8,128)S(1)} %fusion.62, f32[1024,352]{0,1:T(8,128)} %fusion.61), kind=kOutput, calls=%fused_computation.15 | convolution fusion | flops 1735320576 | bytes 9966976 | tf_op jit(solution)/shard_map/dot_general | solution.py:20
  247.9 6.0 %fusion.5 = bf16[1,1,352,2048]{3,2,1,0:T(8,128)(2,1)} fusion(bf16[1024,2048]{0,1:T(8,128)(2,1)} %bitcast.104, f32[1024]{0:T(1024)S(1)} %bitcast.111, f32[1024,352]{0,1:T(8,128)} %fusion.61, s32[352]{0:T(512)S(1)} %fusion.15, f32[1024,352]{0,1:T(8,128)S(1)} %fusion.60), kind=kOutput, calls=%fused_computation.17 | convolution fusion | flops 1733878784 | bytes 8525184 | tf_op jit(solution)/shard_map/dot_general | solution.py:20
  254.0 4.7 %fusion.16 = f32[1024,2048]{1,0:T(8,128)S(1)} fusion(bf16[352,2048]{1,0:T(8,128)(2,1)} %bitcast.97, f32[1024]{0:T(1024)S(1)} %convert_add_fusion, f32[1024,352]{0,1:T(8,128)S(1)} %fusion.60, f32[1024,352]{0,1:T(8,128)S(1)} %fusion.62, f32[1024,352]{0,1:T(8,128)} %fusion.61), kind=kOutput, calls=%fused_computation.41 | convolution fusion | flops 1480359936 | bytes 14159872 | tf_op jit(solution)/shard_map/dot_general | solution.py:20
  258.7 4.8 %convolution_convert_fusion.refs_0_ = bf16[1024,2048]{1,0:T(8,128)(2,1)} fusion(bf16[352,2048]{1,0:T(8,128)(2,1)S(1)} %bitcast.106, f32[1024]{0:T(1024)S(1)} %convert_add_fusion, f32[1024,352]{0,1:T(8,128)S(1)} %copy-done.3, f32[1024,352]{0,1:T(8,128)S(1)} %fusion.60), kind=kOutput, calls=%fused_computation.11 | convolution fusion | flops 1481015296 | bytes 8523776 | tf_op jit(solution)/shard_map/dot_general | solution.py:20
  263.5 4.6 %add_convert_fusion.refs_1_ = bf16[1024,2048]{1,0:T(8,128)(2,1)} fusion(f32[1024,2048]{1,0:T(8,128)S(1)} %fusion.16, bf16[352,2048]{1,0:T(8,128)(2,1)S(1)} %bitcast.95, f32[1024]{0:T(1024)S(1)} %convert_add_fusion, f32[1024,352]{0,1:T(8,128)S(1)} %fusion.62, f32[1024,352]{0,1:T(8,128)S(1)} %fusion.60), kind=kOutput, calls=%fused_computation.3 | convolution fusion | flops 1483112448 | bytes 16912384 | tf_op jit(solution)/shard_map/dot_general | solution.py:20
  268.1 54.7 %halving_sum.1 = (bf16[128,512]{1,0:T(8,128)(2,1)}, bf16[128,512]{1,0:T(8,128)(2,1)}) custom-call(bf16[1024,2048]{1,0:T(8,128)(2,1)} %convolution_convert_fusion.refs_0_, bf16[1024,2048]{1,0:T(8,128)(2,1)} %add_convert_fusion.refs_1_), custom_call_target="tpu_custom_call" | custom-call | tf_op jit(solution)/shard_map/halving_sum/pallas_call | solution.py:182
  322.9 3.4 %pad_maximum_fusion = bf16[1,3,352,2048]{3,2,1,0:T(8,128)(2,1)} fusion(bf16[1,1,352,2048]{3,2,1,0:T(8,128)(2,1)} %fusion.5, bf16[1,1,352,2048]{3,2,1,0:T(8,128)(2,1)S(1)} %copy-done.6, bf16[1,1,352,2048]{3,2,1,0:T(8,128)(2,1)S(1)} %copy-done.7), kind=kLoop, calls=%fused_computation.6 | loop fusion | flops 4325376 | bytes 8650752 | tf_op jit(solution)/shard_map/stack | solution.py:289
  326.3 0.7 copy.64
  327.0 0.7 copy.65
  (30 shorter events, 0.2 us)
Async XLA Ops:
  7.2 11.4 %copy-start.10 = (s32[8]{0:T(128)S(1)}, s32[8]{0:T(128)}, u32[]{:S(2)}) copy-start(s32[8]{0:T(128)} %param.13) | copy-start | bytes 100
  7.2 55.3 %all-gather.4.cloned.1.call-start = ((), (), s32[]{:S(2)}) async-start(), calls=%async_computation.2 | async-start | bytes 2359296 | tf_op jit(solution)/shard_map/all_gather | solution.py:252
  10.3 63.4 %all-to-all-start = ((f32[8,1,128]{2,1,0:T(1,128)}), f32[8,1,128]{2,1,0:T(1,128)S(1)}, u32[]{:S(2)}, u32[]{:S(2)}) async-start(f32[8,1,128]{2,1,0:T(1,128)} %bitcast.1), calls=%async_computation | async-start | bytes 8192 | tf_op jit(solution)/shard_map/all_to_all | solution.py:265
  17.6 188.6 %all-gather.6.cloned.1.call-start = ((), (), s32[]{:S(2)}) async-start(), calls=%async_computation.3 | async-start | bytes 10485760 | tf_op jit(solution)/shard_map/all_gather | solution.py:253
  62.5 1.6 copy-start.4
  73.7 102.2 %all-to-all-start.1 = ((bf16[32,88,768]{2,1,0:T(8,128)(2,1)}), bf16[32,88,768]{2,1,0:T(8,128)(2,1)}, u32[]{:S(2)}, u32[]{:S(2)}) async-start(bf16[32,88,768]{2,1,0:T(8,128)(2,1)} %bitcast.98), calls=%async_computation.1 | async-start | bytes 8650752 | tf_op jit(solution)/shard_map/all_to_all | solution.py:226
  203.8 19.0 %copy-start = (bf16[44,8,8,256]{3,1,2,0:T(8,128)(2,1)}, bf16[44,8,8,256]{3,1,2,0:T(8,128)(2,1)S(1)}, u32[]{:S(2)}) copy-start(bf16[44,8,8,256]{3,1,2,0:T(8,128)(2,1)S(1)} %copy.49) | copy-start | bytes 4325380
  218.4 4.4 %copy-start.2 = (bf16[1024,4,512]{0,2,1:T(8,128)(2,1)S(1)}, bf16[1024,4,512]{0,2,1:T(8,128)(2,1)}, u32[]{:S(2)}) copy-start(bf16[1024,4,512]{0,2,1:T(8,128)(2,1)} %copy.40) | copy-start | bytes 12582916
  254.0 4.7 %copy-start.3 = (f32[1024,352]{0,1:T(8,128)S(1)}, f32[1024,352]{0,1:T(8,128)}, u32[]{:S(2)}) copy-start(f32[1024,352]{0,1:T(8,128)} %fusion.61) | copy-start | bytes 4325380
  254.0 4.7 %copy-start.5 = (bf16[44,8,8,256]{3,1,2,0:T(8,128)(2,1)S(1)}, bf16[44,8,8,256]{3,1,2,0:T(8,128)(2,1)}, u32[]{:S(2)}) copy-start(bf16[44,8,8,256]{3,1,2,0:T(8,128)(2,1)} %copy.50) | copy-start | bytes 4325380
  258.7 4.8 %copy-start.1 = (bf16[44,8,8,256]{3,1,2,0:T(8,128)(2,1)S(1)}, bf16[44,8,8,256]{3,1,2,0:T(8,128)(2,1)}, u32[]{:S(2)}) copy-start(bf16[44,8,8,256]{3,1,2,0:T(8,128)(2,1)} %copy-done) | copy-start | bytes 4325380
  268.1 54.7 %copy-start.6 = (bf16[1,1,352,2048]{3,2,1,0:T(8,128)(2,1)S(1)}, bf16[1,1,352,2048]{3,2,1,0:T(8,128)(2,1)}, u32[]{:S(2)}) copy-start(bf16[1,1,352,2048]{3,2,1,0:T(8,128)(2,1)} %fusion.4) | copy-start | bytes 4325380
  268.1 54.7 %copy-start.7 = (bf16[1,1,352,2048]{3,2,1,0:T(8,128)(2,1)S(1)}, bf16[1,1,352,2048]{3,2,1,0:T(8,128)(2,1)}, u32[]{:S(2)}) copy-start(bf16[1,1,352,2048]{3,2,1,0:T(8,128)(2,1)} %fusion.3) | copy-start | bytes 4325380
  322.9 3.5 %copy-start.9 = (bf16[128,512]{1,0:T(8,128)(2,1)S(1)}, bf16[128,512]{1,0:T(8,128)(2,1)}, u32[]{:S(2)}) copy-start(bf16[128,512]{1,0:T(8,128)(2,1)} %get-tuple-element.22) | copy-start | bytes 393220
  322.9 4.1 %copy-start.8 = (bf16[128,512]{1,0:T(8,128)(2,1)S(1)}, bf16[128,512]{1,0:T(8,128)(2,1)}, u32[]{:S(2)}) copy-start(bf16[128,512]{1,0:T(8,128)(2,1)} %get-tuple-element.23) | copy-start | bytes 393220
Sparse Core Ops, SparseCore 0:
  10.7 51.7 all-gather.3
  64.1 97.5 all-gather.5
